TPU v7x, 32 devices: a whole 2x2x4 slice. The times are simulated.
32 devices in a mesh: tm: 8 (over z, x), state: 4 (over y, core).
Axes of the slice: x: 2, y: 2, z: 4, core: 2. Of those that a mesh axis runs over, the one named last changes fastest.
Arguments:
- dyn_cols: int32 [256, 8, 3], P('tm', 'state'), may hold values from 0 to 7, as said below
- dyn_vals: bfloat16 [256, 8, 64, 192], P('tm', 'state'), may hold values from -1 to 1
- obs_blocks: int32 [256, 2], P('tm'), may hold values from 0 to 7
- obs_op: bfloat16 [256, 64, 128], P('tm'), may hold values from -0.75 to 0.75
- obs_counts: int32 [256], P('tm'), may hold values from 32 to 128, as said below
- obs_values: float32 [256, 128], P('tm'), may hold values from -6 to 6
- gain: bfloat16 [256, 512, 128], P('tm', 'state'), may hold values from -0.0078125 to 0.0078125
- sources: float32 [256, 512], P('tm', 'state'), may hold values from -0.625 to 0.625
- prior: float32 [512], replicated, may hold values from -6 to 6
Outputs:
- filtered: float32 [256, 512], P('tm', 'state')
Inputs may be any that keep to these rules, and one draw needn't show every extreme that they name: `dyn_cols`: for every step and block row i, the first entry is i itself and the 3 entries are distinct block columns. `obs_counts`: some step has all 128 observations present.
All inputs are finite; a program needn't handle non-finite values.
Results may differ from a plain program's by a relative error of at most 0.0003.
The roundings to bfloat16 on the way count: a program that leaves them out, or rounds other values in their place, can miss the bound.
Values may be sent and summed in bfloat16 or wider, within the bound.
No kernel may reach another device: no remote copies, remote signals or barrier semaphores. Data moves between devices by JAX's collectives and lax.ppermute only.
A program may use at most 128 MiB of HBM per device.

v0:
```python
import jax
import jax.numpy as jnp
from jax import lax
from jax.sharding import PartitionSpec as P

NS = 512
BS = 64
KF = 3
OBS = 128
NB = 8
OB = 2
HIGHEST = lax.Precision.HIGHEST


def shifted(shard, axis, by):
    devices = lax.axis_size(axis)
    pairs = [(i, i + by) for i in range(devices) if 0 <= i + by < devices]
    return lax.ppermute(shard, axis, pairs)


def split_product(matrix, operand):
    leading = operand.astype(jnp.bfloat16)
    remainder = (operand - lax.optimization_barrier(leading).astype(jnp.float32)).astype(
        jnp.bfloat16
    )
    return jnp.dot(matrix, leading, preferred_element_type=jnp.float32) + jnp.dot(
        matrix, remainder, preferred_element_type=jnp.float32
    )


def body(dyn_cols, dyn_vals, obs_blocks, obs_op, obs_counts, obs_values, gain, sources, prior):
    step_count = dyn_vals.shape[0]
    local_blocks = dyn_vals.shape[1]
    local_rows = local_blocks * BS
    state_index = lax.axis_index("state")
    time_index = lax.axis_index("tm")
    onehot = (dyn_cols[..., None] == jnp.arange(NB)).astype(jnp.bfloat16)
    blocks = dyn_vals.reshape(step_count, local_blocks, BS, KF, BS)
    forward = jnp.einsum("tikc,tiakb->tiacb", onehot, blocks, preferred_element_type=jnp.float32)
    forward = forward.reshape(step_count, local_blocks, BS, NS)
    forward_narrow = forward.astype(jnp.bfloat16)
    owned = state_index * local_blocks + jnp.arange(local_blocks)
    select = obs_blocks[:, :, None] == owned[None, None, :]
    selected = jnp.einsum(
        "tos,tsbn->tobn",
        select.astype(jnp.bfloat16),
        forward_narrow,
        preferred_element_type=jnp.float32,
    ).astype(jnp.bfloat16)
    operator_blocks = obs_op.reshape(step_count, BS, OB, BS)
    image_part = jnp.einsum(
        "tboa,tobn->toan", operator_blocks, selected, preferred_element_type=jnp.float32
    )
    image_part = image_part.reshape(step_count, OBS, NS)
    source_sel = jnp.einsum(
        "tos,tsb->tob",
        select.astype(jnp.float32),
        sources.reshape(step_count, local_blocks, BS),
        precision=HIGHEST,
    )
    source_part = jnp.einsum(
        "tboa,tob->toa", operator_blocks.astype(jnp.float32), source_sel, precision=HIGHEST
    )
    source_part = source_part.reshape(step_count, OBS)
    image_sum, source_sum = (
        lax.psum(image_part.astype(jnp.bfloat16), "state").astype(jnp.float32),
        lax.psum(source_part.astype(jnp.bfloat16), "state").astype(jnp.float32),
    )
    active = jnp.arange(OBS)[None, :] < obs_counts[:, None]
    masked = jnp.where(
        active[:, :, None], image_sum.astype(jnp.bfloat16), jnp.zeros((), jnp.bfloat16)
    )
    source_image = lax.optimization_barrier(source_sum.astype(jnp.bfloat16)).astype(jnp.float32)
    innovation = jnp.where(active, obs_values - source_image, 0.0)
    correction = jnp.einsum("tro,ton->trn", gain, masked, preferred_element_type=jnp.float32)
    element = (forward.reshape(step_count, local_rows, NS) - correction).astype(jnp.bfloat16)
    offset = sources + jnp.einsum(
        "tro,to->tr", gain.astype(jnp.float32), innovation, precision=HIGHEST
    )
    full_elements = lax.all_gather(element, "state", axis=1, tiled=True)
    full_offsets = lax.all_gather(offset, "state", axis=1, tiled=True)
    start_cols = (
        jnp.arange(NS)[:, None] == (state_index * local_rows + jnp.arange(local_rows))[None, :]
    ).astype(jnp.float32)

    def compose(carry, inputs):
        product, vector = carry
        matrix, shift_term = inputs
        product = split_product(matrix, product)
        vector = split_product(matrix, vector) + shift_term
        return ((product, vector), None)

    (column_product, span_offset), _ = lax.scan(
        compose, (start_cols, jnp.zeros((NS,), jnp.float32)), (full_elements, full_offsets)
    )
    span_matrix = lax.all_gather(column_product, "state", axis=1, tiled=True)
    first_span = time_index == 0

    def hand_over(turn, current):
        leaving = jnp.dot(span_matrix, current, precision=HIGHEST) + span_offset
        arriving = shifted(leaving, "tm", 1)
        return jnp.where(first_span, prior, arriving)

    entry = lax.fori_loop(0, lax.axis_size("tm") - 1, hand_over, prior)

    def sweep(current, inputs):
        matrix, shift_term = inputs
        new_mean = split_product(matrix, current) + shift_term
        return (new_mean, lax.dynamic_slice_in_dim(new_mean, state_index * local_rows, local_rows))

    _, filtered = lax.scan(sweep, entry, (full_elements, full_offsets))
    return filtered


def solution(mesh):
    return jax.shard_map(
        body,
        mesh=mesh,
        in_specs=(
            P("tm", "state", None),
            P("tm", "state", None, None),
            P("tm", None),
            P("tm", None, None),
            P("tm"),
            P("tm", None),
            P("tm", "state", None),
            P("tm", "state"),
            P(),
        ),
        out_specs=P("tm", "state"),
        check_vma=False,
    )
```

profile of v0, /device:TPU:8, one launch (start us, length us, event | category | flops | bytes accessed | tf_op | source)
XLA Modules:
  0.0 674.5 jit_solution(3673502673892375149)
XLA Ops:
  8.2 2.4 reshape.47
  10.6 4.5 copy.18
  15.1 7.1 %copy.19 = bf16[32,2,64,3,64]{4,3,2,1,0:T(4,128)(2,1)} copy(bf16[32,2,64,3,64]{2,4,3,1,0:T(8,128)(2,1)} %bitcast.140) | data formatting | bytes 3145728 | tf_op jit(solution)/shard_map/reshape | solution.py:38
  22.3 10.6 %fusion.48 = (bf16[32,2,64,8,64]{4,3,2,1,0:T(8,128)(2,1)}, f32[32,2,64,8,64]{4,3,2,1,0:T(8,128)}) fusion(bf16[32,2,64,3,64]{4,3,2,1,0:T(4,128)(2,1)} %copy.19, s32[32,2,3]{2,1,0:T(2,128)S(1)} %copy.17), kind=kOutput, calls=%fused_computation.66 | convolution fusion | flops 14681600 | bytes 14156544 | tf_op jit(solution)/shard_map/tikc,tiakb->tiacb/dot_general | solution.py:39
  32.9 11.8 %convert_element_type.77 = bf16[32,2,64,512]{3,2,1,0:T(8,128)(2,1)} reshape(bf16[32,2,64,8,64]{4,3,2,1,0:T(8,128)(2,1)} %get-tuple-element.218) | data formatting | bytes 8388608 | tf_op jit(solution)/shard_map/convert_element_type | solution.py:41
  44.7 8.7 %fusion.28 = bf16[32,2,64,512]{3,1,2,0:T(2,128)(2,1)S(1)} fusion(bf16[32,2,64,512]{3,2,1,0:T(8,128)(2,1)} %convert_element_type.77, s32[2]{0:T(128)S(1)} %iota_add_fusion, s32[32,2]{1,0:T(8,128)S(1)} %copy.20), kind=kOutput, calls=%fused_computation.42 | convolution fusion | flops 8388736 | bytes 8388872 | tf_op jit(solution)/shard_map/tos,tsbn->tobn/dot_general | solution.py:44
  53.5 3.2 fusion.32
  56.7 6.5 copy.22
  63.2 14.5 %reshape_reshape.3 = f32[32,128,512]{2,1,0:T(8,128)} reshape(f32[32,2,64,8,64]{4,3,2,1,0:T(8,128)} %get-tuple-element.219) | data formatting | bytes 16777216 | tf_op jit(solution)/shard_map/reshape;reshape | solution.py:76
  77.7 9.0 %copy.23 = f32[32,128,512]{1,2,0:T(8,128)} copy(f32[32,128,512]{2,1,0:T(8,128)} %reshape_reshape.3) | data formatting | bytes 16777216 | tf_op jit(solution)/shard_map/reshape;reshape | solution.py:76
  86.8 63.2 %all-reduce.2.cloned.1.call-done = bf16[32,128,512]{1,2,0:T(8,128)(2,1)} async-done(((bf16[32,128,512]{1,2,0:T(8,128)(2,1)}), bf16[32,128,512]{1,2,0:T(8,128)(2,1)}) %all-reduce.2.cloned.1.call-update) | async-done | bytes 4194320 | tf_op jit(solution)/shard_map/psum | solution.py:66
  150.0 7.9 %fusion.23 = bf16[32,128,512]{1,2,0:T(8,128)(2,1)} fusion(f32[32,128,512]{1,2,0:T(8,128)} %copy.23, bf16[32,128,128]{2,1,0:T(8,128)(2,1)S(1)} %copy-done, bf16[32,128,512]{1,2,0:T(8,128)(2,1)} %all-reduce.2.cloned.1.call-done, pred[32,128]{1,0:T(8,128)(4,1)S(1)} %iota_compare_fusion.2), kind=kOutput, calls=%fused_computation.36 | convolution fusion | flops 543162368 | bytes 17829888 | tf_op jit(solution)/shard_map/tro,ton->trn/dot_general | solution.py:75
  160.0 6.4 psum.15
  166.5 1.7 fusion.50
  168.3 5.5 all_gather.10
  173.8 92.7 %all-gather.3.cloned.1.call-done = bf16[32,512,512]{1,2,0:T(8,128)(2,1)} async-done(((bf16[32,128,512]{1,2,0:T(8,128)(2,1)}), bf16[32,512,512]{1,2,0:T(8,128)(2,1)}) %all-gather.3.cloned.1.call-update) | async-done | bytes 16777232 | tf_op jit(solution)/shard_map/all_gather | solution.py:80
  266.5 22.5 %copy.24 = bf16[32,512,512]{2,1,0:T(8,128)(2,1)} copy(bf16[32,512,512]{1,2,0:T(8,128)(2,1)} %all-gather.3.cloned.1.call-done) | data formatting | bytes 33554432
  289.1 173.2 %while.42 = (s32[]{:T(128)}, f32[512,128]{1,0:T(8,128)S(1)}, f32[512]{0:T(512)S(1)}, bf16[32,512,512]{2,1,0:T(8,128)(2,1)}, f32[32,512]{1,0:T(8,128)S(1)}) while((s32[]{:T(128)}, f32[512,128]{1,0:T(8,128)S(1)}, f32[512]{0:T(512)S(1)}, bf16[32,512,512]{2,1,0:T(8,128)(2,1)}, f32[32,512]{1,0:T(8,128)S(1)}) %tuple.69), condition=%wide.region_3.4_spmd.clone.clone, body=%wide.region_2.3_spmd.clone.sunk.clone | while | flops 135597568 | bytes 4355172 | solution.py:93
  293.1 1.4 convolution_add_fusion.3
  298.5 1.3 convolution_add_fusion.3
  303.9 1.3 convolution_add_fusion.3
  309.3 1.3 convolution_add_fusion.3
  314.7 1.3 convolution_add_fusion.3
  331.0 1.3 convolution_add_fusion.3
  463.1 16.9 %all-gather.5.cloned.1.call-done = f32[512,512]{1,0:T(8,128)} async-done(((f32[512,128]{1,0:T(8,128)}), f32[512,512]{1,0:T(8,128)}) %all-gather.5.cloned.1.call-update) | async-done | bytes 1048592 | tf_op jit(solution)/shard_map/all_gather | solution.py:96
  480.0 60.1 %while.40 = (s32[]{:T(128)}, f32[512]{0:T(512)S(1)}, pred[]{:T(512)}, f32[512,512]{1,0:T(8,128)}, f32[512]{0:T(512)S(1)}, /*index=5*/f32[512]{0:T(512)S(1)}) while((s32[]{:T(128)}, f32[512]{0:T(512)S(1)}, pred[]{:T(512)}, f32[512,512]{1,0:T(8,128)}, f32[512]{0:T(512)S(1)}, /*index=5*/f32[512]{0:T(512)S(1)}) %tuple.86), condition=%wide.region_5.6_spmd.clone, body=%wide.region_4.5_spmd.sunk.clone | while | flops 3146754 | bytes 1073262 | solution.py:104
  480.0 2.2 fusion.104
  482.2 3.4 collective-permute-start
  485.6 3.0 collective-permute-done
  488.6 2.2 fusion.104
  490.8 2.5 collective-permute-start
  493.3 3.9 collective-permute-done
  497.2 2.2 fusion.104
  499.4 1.9 collective-permute-start
  501.3 4.4 collective-permute-done
  505.8 2.2 fusion.104
  508.0 1.9 collective-permute-start
  509.9 4.4 collective-permute-done
  514.4 2.2 fusion.104
  516.6 1.9 collective-permute-start
  518.5 4.4 collective-permute-done
  523.0 2.2 fusion.104
  525.2 1.9 collective-permute-start
  527.1 4.4 collective-permute-done
  531.6 2.2 fusion.104
  533.8 1.9 collective-permute-start
  535.7 4.4 collective-permute-done
  540.2 127.8 %while.41 = (s32[]{:T(128)}, f32[512]{0:T(512)S(1)}, f32[32,128]{1,0:T(8,128)}, bf16[32,512,512]{2,1,0:T(8,128)(2,1)}, f32[32,512]{1,0:T(8,128)S(1)}, /*index=5*/s32[]{:T(128)}) while((s32[]{:T(128)}, f32[512]{0:T(512)S(1)}, f32[32,128]{1,0:T(8,128)}, bf16[32,512,512]{2,1,0:T(8,128)(2,1)}, f32[32,512]{1,0:T(8,128)S(1)}, ...), condition=%wide.region_7.8_spmd.clone, body=%wide.region_6.7_spmd.sunk.clone | while | flops 1051650 | bytes 1080417 | solution.py:111
  (746 shorter events, 295.0 us)
Async XLA Ops:
  6.5 143.4 %copy-start = (bf16[32,128,128]{2,1,0:T(8,128)(2,1)S(1)}, bf16[32,128,128]{2,1,0:T(8,128)(2,1)}, u32[]{:S(2)}) copy-start(bf16[32,128,128]{2,1,0:T(8,128)(2,1)} %param.21) | copy-start | bytes 3145732
  6.5 143.4 %all-reduce.2.cloned.1.call-start = ((), (), s32[]{:S(2)}) async-start(), calls=%async_computation | async-start | bytes 8388608 | tf_op jit(solution)/shard_map/psum | solution.py:66
  63.2 203.3 %all-gather.3.cloned.1.call-start = ((), (), s32[]{:S(2)}) async-start(), calls=%async_computation.1 | async-start | bytes 20971520 | tf_op jit(solution)/shard_map/all_gather | solution.py:80
  77.7 9.0 %copy-start.5 = (s32[32]{0:T(128)S(1)}, s32[32]{0:T(128)}, u32[]{:S(2)}) copy-start(s32[32]{0:T(128)} %param.19) | copy-start | bytes 388
  157.9 0.7 copy-start.3
  157.9 8.6 %copy-start.4 = (f32[32,128]{1,0:T(8,128)S(1)}, f32[32,128]{1,0:T(8,128)}, u32[]{:S(2)}) copy-start(f32[32,128]{1,0:T(8,128)} %param.20) | copy-start | bytes 49156
  157.9 322.1 %all-gather.5.cloned.1.call-start = ((), (), s32[]{:S(2)}) async-start(), calls=%async_computation.2 | async-start | bytes 1310720 | tf_op jit(solution)/shard_map/all_gather | solution.py:96
  289.1 174.0 %copy-start.2 = (f32[512]{0:T(512)S(1)}, f32[512]{0:T(512)}, u32[]{:S(2)}) copy-start(f32[512]{0:T(512)} %param.23) | copy-start | bytes 6148
  462.3 0.7 copy-start.1
  482.2 6.4 collective-permute-start
  490.8 6.4 collective-permute-start
  499.4 6.4 collective-permute-start
  508.0 6.4 collective-permute-start
  516.6 6.4 collective-permute-start
  525.2 6.4 collective-permute-start
  533.8 6.4 collective-permute-start
Sparse Core Ops, SparseCore 0:
  63.3 86.6 all-reduce.1
  158.0 108.4 all-gather.2
  463.2 16.8 all-gather.4
where the time goes:
time: 687 us; the launch traced here: 674 us
  matrix products  299 us (44%)
  waiting for transfers between devices  202 us (29%)
  local copies, waits for them, and re-layouts  127 us (18%)
  starting transfers between devices  15.6 us (2%)
  between operations  13.2 us (2%)
  blocking collectives  11.9 us (2%)
    dot_general x96, matrix products, split_product(): jnp.dot(matrix, leading, preferred_element_type=jnp.float32)  126 us
    dot_general x96, matrix products, split_product(): jnp.dot(matrix, remainder, preferred_element_type=jnp.float32)  125 us
    all_gather x1, waiting for transfers between devices, body(): full_elements = lax.all_gather(element, 'state', axis=1, tiled=True)  92.7 us
    psum x1, waiting for transfers between devices, body(): lax.psum(image_part.astype(jnp.bfloat16), 'state').astype(jnp.float32)  63.2 us
    dynamic_update_slice x32, local copies, waits for them, and re-layouts, body(): _, filtered = lax.scan(sweep, entry, (full_elements, full_offsets))  41.3 us
    unnamed x17, local copies, waits for them, and re-layouts  30 us
    ppermute x7, waiting for transfers between devices, shifted(): return lax.ppermute(shard, axis, pairs)  29.1 us
    another operation x2, local copies, waits for them, and re-layouts, body(): forward.reshape(step_count, local_rows, NS) - correction  23.5 us
  transfers between devices with their start and end apart: 10, of which 10 were waited for; matrix products, arithmetic and copies ran while one was open for 4% of the time, Pallas kernels for 0%

commit v1 on v0

--- a/solution.py
+++ b/solution.py
@@ -77,7 +77,9 @@
     offset = sources + jnp.einsum(
         "tro,to->tr", gain.astype(jnp.float32), innovation, precision=HIGHEST
     )
-    full_elements = lax.all_gather(element, "state", axis=1, tiled=True)
+    full_elements = jnp.concatenate(
+        lax.all_to_all(jnp.stack([element] * lax.axis_size("state")), "state", 0, 0), axis=1
+    )
     full_offsets = lax.all_gather(offset, "state", axis=1, tiled=True)
     start_cols = (
         jnp.arange(NS)[:, None] == (state_index * local_rows + jnp.arange(local_rows))[None, :]

time: 687 us -> 784 us (1.14)
  blocking collectives: 11.9 us -> 188 us
  waiting for transfers between devices: 202 us -> 110 us
    psum x1, blocking collectives: 6.43 us -> 183 us  [body(): lax.psum(source_part.astype(jnp.bfloat16), 'state').astype(jnp.float32)]
    all_gather x1 -> x0, waiting for transfers between devices: 92.7 us -> none  [body(): full_elements = lax.all_gather(element, 'state', axis=1, tiled=True)]
    unnamed x17 -> x16, local copies, waits for them, and re-layouts: 30 us -> 6.85 us
    all_to_all x0 -> x1, local copies, waits for them, and re-layouts: none -> 13.9 us  [body(): lax.all_to_all(jnp.stack([element] * lax.axis_size('state')), 'state', 0, 0)]
  transfers between devices with their start and end apart: 10 -> 10, of which waited for: 10 -> 9; matrix products, arithmetic and copies ran while one was open for 4% -> 3% of each run, Pallas kernels for 0% -> 0%
where the time goes in v1:
time: 784 us; the launch traced here: 771 us
  matrix products  299 us (38%)
  blocking collectives  188 us (24%)
  local copies, waits for them, and re-layouts  132 us (17%)
  waiting for transfers between devices  110 us (14%)
  starting transfers between devices  22.8 us (3%)
  between operations  13.6 us (2%)
    psum x1, blocking collectives, body(): lax.psum(source_part.astype(jnp.bfloat16), 'state').astype(jnp.float32)  183 us
    dot_general x96, matrix products, split_product(): jnp.dot(matrix, leading, preferred_element_type=jnp.float32)  126 us
    dot_general x96, matrix products, split_product(): jnp.dot(matrix, remainder, preferred_element_type=jnp.float32)  125 us
    psum x1, waiting for transfers between devices, body(): lax.psum(image_part.astype(jnp.bfloat16), 'state').astype(jnp.float32)  63.2 us
    dynamic_update_slice x32, local copies, waits for them, and re-layouts, body(): _, filtered = lax.scan(sweep, entry, (full_elements, full_offsets))  41.3 us
    ppermute x7, waiting for transfers between devices, shifted(): return lax.ppermute(shard, axis, pairs)  29.1 us
    another operation x2, local copies, waits for them, and re-layouts, body(): forward.reshape(step_count, local_rows, NS) - correction  23.5 us
    all_gather x1, waiting for transfers between devices, body(): span_matrix = lax.all_gather(column_product, 'state', axis=1, tiled=True)  18 us
  transfers between devices with their start and end apart: 10, of which 9 were waited for; matrix products, arithmetic and copies ran while one was open for 3% of the time, Pallas kernels for 0%

profile of v1, /device:TPU:8, one launch (start us, length us, event | category | flops | bytes accessed | tf_op | source)
XLA Modules:
  0.0 771.2 jit_solution(16532251579400438252)
XLA Ops:
  8.2 2.4 reshape.55
  10.6 4.5 copy.35
  15.1 7.1 copy.36
  22.3 10.6 %fusion.50 = (bf16[32,2,64,8,64]{4,3,2,1,0:T(8,128)(2,1)}, f32[32,2,64,8,64]{4,3,2,1,0:T(8,128)}) fusion(bf16[32,2,64,3,64]{4,3,2,1,0:T(4,128)(2,1)} %copy.36, s32[32,2,3]{2,1,0:T(2,128)S(1)} %copy.34), kind=kOutput, calls=%fused_computation.66 | convolution fusion | flops 14681600 | bytes 14156544 | tf_op jit(solution)/shard_map/tikc,tiakb->tiacb/dot_general | solution.py:39
  32.9 11.8 %convert_element_type.77 = bf16[32,2,64,512]{3,2,1,0:T(8,128)(2,1)} reshape(bf16[32,2,64,8,64]{4,3,2,1,0:T(8,128)(2,1)} %get-tuple-element.196) | data formatting | bytes 8388608 | tf_op jit(solution)/shard_map/convert_element_type | solution.py:41
  44.7 8.7 %convolution_convert_fusion = bf16[32,2,64,512]{3,1,2,0:T(2,128)(2,1)S(1)} fusion(bf16[32,2,64,512]{3,2,1,0:T(8,128)(2,1)} %convert_element_type.77, s32[2]{0:T(128)S(1)} %iota_add_fusion, s32[32,2]{1,0:T(8,128)S(1)} %copy.37), kind=kOutput, calls=%fused_computation.37 | convolution fusion | flops 10485888 | bytes 8388872 | tf_op jit(solution)/shard_map/tos,tsbn->tobn/dot_general | solution.py:44
  53.4 3.2 fusion.32
  56.7 6.4 copy.41
  63.1 14.5 %reshape_reshape.3 = f32[32,128,512]{2,1,0:T(8,128)} reshape(f32[32,2,64,8,64]{4,3,2,1,0:T(8,128)} %get-tuple-element.197) | data formatting | bytes 16777216 | tf_op jit(solution)/shard_map/reshape;reshape | solution.py:76
  77.6 9.0 %copy.42 = f32[32,128,512]{1,2,0:T(8,128)} copy(f32[32,128,512]{2,1,0:T(8,128)} %reshape_reshape.3) | data formatting | bytes 16777216 | tf_op jit(solution)/shard_map/reshape;reshape | solution.py:76
  86.7 63.2 %all-reduce.2.cloned.1.call-done = bf16[32,128,512]{1,2,0:T(8,128)(2,1)} async-done(((bf16[32,128,512]{1,2,0:T(8,128)(2,1)}), bf16[32,128,512]{1,2,0:T(8,128)(2,1)}) %all-reduce.2.cloned.1.call-update) | async-done | bytes 4194320 | tf_op jit(solution)/shard_map/psum | solution.py:66
  149.9 7.9 %fusion.23 = bf16[32,128,512]{1,2,0:T(8,128)(2,1)} fusion(f32[32,128,512]{1,2,0:T(8,128)} %copy.42, bf16[32,128,128]{2,1,0:T(8,128)(2,1)S(1)} %copy-done, bf16[32,128,512]{1,2,0:T(8,128)(2,1)} %all-reduce.2.cloned.1.call-done, pred[32,128]{1,0:T(8,128)(4,1)S(1)} %iota_compare_fusion.2), kind=kOutput, calls=%fused_computation.36 | convolution fusion | flops 543162368 | bytes 17829888 | tf_op jit(solution)/shard_map/tro,ton->trn/dot_general | solution.py:75
  157.8 6.5 copy.43
  164.3 7.4 stack.2
  171.7 7.1 all-to-all-start
  180.5 182.9 %psum.15 = bf16[32,128]{1,0:T(8,128)(2,1)S(1)} all-reduce(bf16[32,128]{1,0:T(8,128)(2,1)S(1)} %convert_element_type.84), channel_id=1, replica_groups=mesh['tm'=8,'state'=4] {'state'}, use_global_device_ids=true, to_apply=%region_1.0 | all-reduce | flops 4096 | bytes 16384 | tf_op jit(solution)/shard_map/psum | solution.py:67
  363.5 1.7 fusion.52
  365.2 5.2 all_gather.6
  370.5 13.9 %copy.44 = bf16[4,32,128,512]{3,2,0,1:T(8,128)(2,1)} copy(bf16[4,32,128,512]{3,2,1,0:T(8,128)(2,1)} %all-to-all-done) | data formatting | bytes 33554432 | tf_op jit(solution)/shard_map/all_to_all | solution.py:81
  384.4 173.2 %while.42 = (s32[]{:T(128)}, f32[512,128]{1,0:T(8,128)S(1)}, f32[512]{0:T(512)S(1)}, bf16[32,512,512]{2,1,0:T(8,128)(2,1)}, f32[32,512]{1,0:T(8,128)S(1)}) while((s32[]{:T(128)}, f32[512,128]{1,0:T(8,128)S(1)}, f32[512]{0:T(512)S(1)}, bf16[32,512,512]{2,1,0:T(8,128)(2,1)}, f32[32,512]{1,0:T(8,128)S(1)}) %tuple.78), condition=%wide.region_3.4_spmd.clone.clone, body=%wide.region_2.3_spmd.clone.sunk.clone | while | flops 135597568 | bytes 4355172 | solution.py:95
  393.8 1.3 convolution_add_fusion.3
  399.2 1.3 convolution_add_fusion.3
  404.7 1.3 convolution_add_fusion.3
  415.5 1.3 convolution_add_fusion.3
  558.4 18.0 %all-gather.2.cloned.1.call-done = f32[512,512]{1,0:T(8,128)} async-done(((f32[512,128]{1,0:T(8,128)}), f32[512,512]{1,0:T(8,128)}) %all-gather.2.cloned.1.call-update) | async-done | bytes 1048592 | tf_op jit(solution)/shard_map/all_gather | solution.py:98
  576.4 60.1 %while.40 = (s32[]{:T(128)}, f32[512]{0:T(512)S(1)}, pred[]{:T(512)}, f32[512,512]{1,0:T(8,128)}, f32[512]{0:T(512)S(1)}, /*index=5*/f32[512]{0:T(512)S(1)}) while((s32[]{:T(128)}, f32[512]{0:T(512)S(1)}, pred[]{:T(512)}, f32[512,512]{1,0:T(8,128)}, f32[512]{0:T(512)S(1)}, /*index=5*/f32[512]{0:T(512)S(1)}) %tuple.81), condition=%wide.region_5.6_spmd.clone, body=%wide.region_4.5_spmd.sunk.clone | while | flops 3146754 | bytes 1073262 | solution.py:106
  576.4 2.2 fusion.106
  578.6 3.4 collective-permute-start
  582.0 3.0 collective-permute-done
  585.0 2.2 fusion.106
  587.2 2.5 collective-permute-start
  589.7 3.9 collective-permute-done
  593.6 2.2 fusion.106
  595.8 1.9 collective-permute-start
  597.7 4.4 collective-permute-done
  602.2 2.2 fusion.106
  604.4 1.9 collective-permute-start
  606.3 4.4 collective-permute-done
  610.8 2.2 fusion.106
  613.0 1.9 collective-permute-start
  614.9 4.4 collective-permute-done
  619.4 2.2 fusion.106
  621.6 1.9 collective-permute-start
  623.5 4.4 collective-permute-done
  628.0 2.2 fusion.106
  630.2 1.9 collective-permute-start
  632.1 4.4 collective-permute-done
  636.6 127.8 %while.41 = (s32[]{:T(128)}, f32[512]{0:T(512)S(1)}, f32[32,128]{1,0:T(8,128)}, bf16[32,512,512]{2,1,0:T(8,128)(2,1)}, f32[32,512]{1,0:T(8,128)S(1)}, /*index=5*/s32[]{:T(128)}) while((s32[]{:T(128)}, f32[512]{0:T(512)S(1)}, f32[32,128]{1,0:T(8,128)}, bf16[32,512,512]{2,1,0:T(8,128)(2,1)}, f32[32,512]{1,0:T(8,128)S(1)}, ...), condition=%wide.region_7.8_spmd.clone, body=%wide.region_6.7_spmd.sunk.clone | while | flops 1051650 | bytes 1080417 | solution.py:113
  (747 shorter events, 297.2 us)
Async XLA Ops:
  6.5 143.4 %copy-start = (bf16[32,128,128]{2,1,0:T(8,128)(2,1)S(1)}, bf16[32,128,128]{2,1,0:T(8,128)(2,1)}, u32[]{:S(2)}) copy-start(bf16[32,128,128]{2,1,0:T(8,128)(2,1)} %param.21) | copy-start | bytes 3145732
  6.5 143.4 %all-reduce.2.cloned.1.call-start = ((), (), s32[]{:S(2)}) async-start(), calls=%async_computation.1 | async-start | bytes 8388608 | tf_op jit(solution)/shard_map/psum | solution.py:66
  77.6 9.0 %copy-start.5 = (s32[32]{0:T(128)S(1)}, s32[32]{0:T(128)}, u32[]{:S(2)}) copy-start(s32[32]{0:T(128)} %param.19) | copy-start | bytes 388
  171.7 7.4 copy-start.3
  171.7 191.7 %copy-start.4 = (f32[32,128]{1,0:T(8,128)S(1)}, f32[32,128]{1,0:T(8,128)}, u32[]{:S(2)}) copy-start(f32[32,128]{1,0:T(8,128)} %param.20) | copy-start | bytes 49156
  171.7 198.8 %all-to-all-start = ((bf16[4,32,128,512]{3,2,1,0:T(8,128)(2,1)}), bf16[4,32,128,512]{3,2,1,0:T(8,128)(2,1)}, u32[]{:S(2)}, u32[]{:S(2)}) async-start(bf16[4,32,128,512]{3,2,1,0:T(8,128)(2,1)} %stack.2), calls=%async_computation | async-start | bytes 33554432 | tf_op jit(solution)/shard_map/all_to_all | solution.py:81
  178.8 397.6 %all-gather.2.cloned.1.call-start = ((), (), s32[]{:S(2)}) async-start(), calls=%async_computation.2 | async-start | bytes 1310720 | tf_op jit(solution)/shard_map/all_gather | solution.py:98
  384.4 174.0 %copy-start.2 = (f32[512]{0:T(512)S(1)}, f32[512]{0:T(512)}, u32[]{:S(2)}) copy-start(f32[512]{0:T(512)} %param.23) | copy-start | bytes 6148
  557.6 0.7 copy-start.1
  578.6 6.4 collective-permute-start
  587.2 6.4 collective-permute-start
  595.8 6.4 collective-permute-start
  604.4 6.4 collective-permute-start
  613.0 6.4 collective-permute-start
  621.6 6.4 collective-permute-start
  630.2 6.4 collective-permute-start
Sparse Core Ops, SparseCore 0:
  63.2 86.6 all-reduce.1
  558.5 17.8 all-gather.1
